TPU v7x, 128 devices: a whole 4x4x4 slice. The times are simulated.
128 devices in a mesh: ctx: 32 (over z, y_lo, x), grp: 4 (over y_hi, core).
Axes of the slice: x: 4, y: 4 (y_hi: 2, y_lo: 2; y = y_hi * 2 + y_lo), z: 4, core: 2. Of those that a mesh axis runs over, the one named last changes fastest.
Arguments:
- query_input: bfloat16 [16384, 4096], P(('ctx', 'grp')), may hold values from -6 to 6
- key_input: bfloat16 [16384, 4096], P(('ctx', 'grp')), may hold values from -6 to 6
- value_input: bfloat16 [16384, 4096], P(('ctx', 'grp')), may hold values from -6 to 6
- out_grad: bfloat16 [16384, 4096], P(('ctx', 'grp')), may hold values from -6 to 6
- residues: float32 [8, 16], replicated, may hold values from -2 to 2
- decay_rates: float32 [8, 16], replicated, may hold values from 3.0517578e-06 to 0.15
Outputs:
- output: float32 [16384, 4096], P(('ctx', 'grp'))
- query_grad: float32 [16384, 4096], P(('ctx', 'grp'))
- key_grad: float32 [16384, 4096], P(('ctx', 'grp'))
- value_grad: float32 [16384, 4096], P(('ctx', 'grp'))
- residue_grad: float32 [8, 16], replicated
All inputs are finite; a program needn't handle non-finite values.
Results may differ from a plain program's by a relative error of at most 0.0055.
Values may be sent and summed in bfloat16 or wider, within the bound.
A program may use at most 192 MiB of HBM per device.

v0:
```python
import math
import jax
import jax.numpy as jnp
from jax import lax
from jax.sharding import PartitionSpec as P

GROUP = 512
HIGHEST = lax.Precision.HIGHEST


def entering(part, axis, combine, identity, reverse):
    count = lax.axis_size(axis)
    place = lax.axis_index(axis)
    ahead = count - 1 - place if reverse else place
    gathered = jax.tree.map(lambda a: lax.all_gather(a, axis), part)
    state = jax.tree.map(lambda a, e: jnp.zeros_like(a) + jnp.asarray(e, a.dtype), part, identity)

    def one(hop, state):
        source = count - 1 - hop if reverse else hop
        return combine(
            state, jax.tree.map(lambda a: lax.dynamic_index_in_dim(a, source, 0, False), gathered)
        )

    return lax.fori_loop(0, ahead, one, state)


def mode_tables(term_residues, decays, pairing, span):
    position = jnp.arange(span).astype(jnp.float32)
    distance = position[:, None] - position[None, :]
    causal_mask = distance >= 0.0
    lag_values = jnp.maximum(distance, 0.0)
    group_count = term_residues.shape[0]

    def one_mode(total, columns):
        res_column, decay_column = columns
        weight = jnp.where(
            causal_mask[None], jnp.exp(-decay_column[:, None, None] * lag_values[None]), 0.0
        )
        total = total + res_column[:, None, None] * weight
        return (total, jnp.sum(pairing * weight, axis=(1, 2)))

    start_total = jnp.zeros((group_count, span, span), jnp.float32)
    causal, inside = lax.scan(one_mode, start_total, (term_residues.T, decays.T))
    upper_part = causal.astype(jnp.bfloat16)
    lower_part = (causal - upper_part.astype(jnp.float32)).astype(jnp.bfloat16)
    return (upper_part, lower_part, inside.T)


def link_states(earlier, later):
    return (later[1][:, :, None] * earlier[0] + later[0], earlier[1] * later[1])


def convolve(product, inner_grad, term_residues, decays, carry_states):
    span, columns = product.shape
    group_count = columns // GROUP
    grouped = product.reshape(span, group_count, GROUP)
    grad_rows = inner_grad.reshape(span, group_count, GROUP)
    pairing = jnp.einsum("agc,bgc->gab", grad_rows, grouped, preferred_element_type=jnp.float32)
    upper_part, lower_part, inside = mode_tables(term_residues, decays, pairing, span)
    mixed_sum = jnp.einsum("gab,bgc->agc", upper_part, grouped, preferred_element_type=jnp.float32)
    mixed_sum = mixed_sum + jnp.einsum(
        "gab,bgc->agc", lower_part, grouped, preferred_element_type=jnp.float32
    )
    conv_sum = jnp.einsum("gab,agc->bgc", upper_part, grad_rows, preferred_element_type=jnp.float32)
    conv_sum = conv_sum + jnp.einsum(
        "gab,agc->bgc", lower_part, grad_rows, preferred_element_type=jnp.float32
    )
    position = jnp.arange(span).astype(jnp.float32)
    to_end = jnp.exp(-decays[:, :, None] * (span - 1.0 - position)[None, None, :])
    from_start = jnp.exp(-decays[:, :, None] * position[None, None, :])
    end_states = jnp.einsum("gmb,bgc->gmc", to_end, grouped.astype(jnp.float32), precision=HIGHEST)
    start_states = jnp.einsum(
        "gma,agc->gmc", from_start, grad_rows.astype(jnp.float32), precision=HIGHEST
    )
    factor = jnp.exp(-decays * float(span))
    carried_in, behind = carry_states(end_states, start_states, factor, span)
    rising = jnp.exp(-decays[:, :, None] * (position + 1.0)[None, None, :])
    falling = jnp.exp(-decays[:, :, None] * (span - position)[None, None, :])
    mixed_sum = mixed_sum + jnp.einsum(
        "gma,gmc->agc", term_residues[:, :, None] * rising, carried_in, precision=HIGHEST
    )
    conv_sum = conv_sum + jnp.einsum(
        "gmb,gmc->bgc", term_residues[:, :, None] * falling, behind, precision=HIGHEST
    )
    projected = jnp.einsum(
        "agc,gmc->gma", grad_rows.astype(jnp.float32), carried_in, precision=HIGHEST
    )
    residue_share = inside + jnp.sum(projected * rising, axis=2)
    return (mixed_sum.reshape(span, columns), conv_sum.reshape(span, columns), residue_share)


def finish(query_part, key_part, value_part, grad_part, mixed_out, conv_grad):
    output = query_part.astype(jnp.float32) * mixed_out
    query_grad = grad_part.astype(jnp.float32) * mixed_out
    key_grad = conv_grad * value_part.astype(jnp.float32)
    value_grad = conv_grad * key_part.astype(jnp.float32)
    return (output, query_grad, key_grad, value_grad)


def gated_inputs(query_input, key_input, value_input, out_grad):
    product = (key_input.astype(jnp.float32) * value_input.astype(jnp.float32)).astype(jnp.bfloat16)
    inner_grad = (out_grad.astype(jnp.float32) * query_input.astype(jnp.float32)).astype(
        jnp.bfloat16
    )
    return (product, inner_grad)


def channel_layout(query_input, key_input, value_input, out_grad, residues, decay_rates):
    product, inner_grad = gated_inputs(query_input, key_input, value_input, out_grad)
    prod_cols, grad_cols = (
        lax.all_to_all(product, "grp", split_axis=1, concat_axis=0, tiled=True),
        lax.all_to_all(inner_grad, "grp", split_axis=1, concat_axis=0, tiled=True),
    )
    row_count, columns = prod_cols.shape
    group_count = columns // GROUP
    first_group = lax.axis_index("grp") * group_count
    local_res = lax.dynamic_slice_in_dim(residues, first_group, group_count, 0)
    local_decay = lax.dynamic_slice_in_dim(decay_rates, first_group, group_count, 0)

    def carry_states(end_states, start_states, factor, span):
        neutral = (jnp.zeros_like(end_states), jnp.ones_like(factor))
        carried_in, spent_ahead = entering((end_states, factor), "ctx", link_states, neutral, False)
        behind, spent_behind = entering((start_states, factor), "ctx", link_states, neutral, True)
        return (carried_in, behind)

    mixed_cols, conv_cols, residue_share = convolve(
        prod_cols, grad_cols, local_res, local_decay, carry_states
    )
    mixed_rows, conv_rows = (
        lax.all_to_all(mixed_cols, "grp", split_axis=0, concat_axis=1, tiled=True),
        lax.all_to_all(conv_cols, "grp", split_axis=0, concat_axis=1, tiled=True),
    )
    results = finish(query_input, key_input, value_input, out_grad, mixed_rows, conv_rows)
    placed = lax.dynamic_update_slice_in_dim(
        jnp.zeros(residues.shape, jnp.float32), residue_share, first_group, 0
    )
    return (results, placed, row_count * lax.axis_size("ctx"))


def on_device(query_input, key_input, value_input, out_grad, residues, decay_rates):
    results, placed, length = channel_layout(
        query_input, key_input, value_input, out_grad, residues, decay_rates
    )
    summed = lax.psum(placed, ("ctx", "grp"))
    residue_grad = summed / (length * math.sqrt(GROUP))
    return (results[0], results[1], results[2], results[3], residue_grad)


def solution(mesh):
    in_specs = (
        P(("ctx", "grp"), None),
        P(("ctx", "grp"), None),
        P(("ctx", "grp"), None),
        P(("ctx", "grp"), None),
        P(),
        P(),
    )
    out_specs = (
        P(("ctx", "grp"), None),
        P(("ctx", "grp"), None),
        P(("ctx", "grp"), None),
        P(("ctx", "grp"), None),
        P(),
    )
    return jax.shard_map(
        on_device, mesh=mesh, in_specs=in_specs, out_specs=out_specs, check_vma=False
    )
```

profile of v0, /device:TPU:1, one launch (start us, length us, event | category | flops | bytes accessed | tf_op | source)
XLA Modules:
  0.0 491.0 jit_solution(2044057091201564266)
XLA Ops:
  7.2 1.8 fusion.5
  9.0 1.1 copy.101
  10.0 6.0 %all-to-all-start.1 = ((bf16[128,4,1024]{2,0,1:T(8,128)(2,1)}), bf16[128,4,1024]{2,0,1:T(8,128)(2,1)S(1)}, u32[]{:S(2)}, u32[]{:S(2)}) async-start(bf16[128,4,1024]{2,0,1:T(8,128)(2,1)} %bitcast.53), calls=%async_computation.1 | async-start | bytes 2097152 | tf_op jit(solution)/shard_map/all_to_all | solution.py:112
  16.9 14.2 %all-to-all-done.1 = bf16[128,4,1024]{2,0,1:T(8,128)(2,1)S(1)} async-done(((bf16[128,4,1024]{2,0,1:T(8,128)(2,1)}), bf16[128,4,1024]{2,0,1:T(8,128)(2,1)S(1)}, u32[]{:S(2)}, u32[]{:S(2)}) %all-to-all-start.1) | async-done | bytes 1048608 | tf_op jit(solution)/shard_map/all_to_all | solution.py:112
  31.1 1.0 copy-done.7
  32.1 1.8 reshape.76
  33.9 1.2 fusion.12
  35.4 1.1 copy.102
  36.5 5.1 %all-to-all-start = ((bf16[128,4,1024]{2,0,1:T(8,128)(2,1)}), bf16[128,4,1024]{2,0,1:T(8,128)(2,1)}, u32[]{:S(2)}, u32[]{:S(2)}) async-start(bf16[128,4,1024]{2,0,1:T(8,128)(2,1)} %bitcast.54), calls=%async_computation | async-start | bytes 2097152 | tf_op jit(solution)/shard_map/all_to_all | solution.py:111
  41.7 68.3 %all-gather.3 = f32[32,2,16]{2,1,0:T(2,128)S(1)} all-gather(f32[1,2,16]{2,1,0:T(2,128)S(1)} %get-tuple-element.293), channel_id=2, replica_groups=mesh['ctx'=32,'grp'=4] {'ctx'}, dimensions={0}, use_global_device_ids=true | all-gather | bytes 4224 | tf_op jit(solution)/shard_map/all_gather | solution.py:15
  110.1 2.6 reshape.75
  112.7 2.4 fusion.7
  115.1 3.3 fusion.9
  118.4 54.7 %while.43 = (s32[]{:T(128)}, f32[2,512,512]{2,1,0:T(8,128)S(1)}, f32[16,2]{1,0:T(8,128)S(1)}, f32[16,2]{1,0:T(8,128)S(1)}, f32[16,2]{1,0:T(8,128)S(1)}, /*index=...) while((s32[]{:T(128)}, f32[2,512,512]{2,1,0:T(8,128)S(1)}, ...), condition=%wide.region_2.3_spmd.clone.clone.clone, body=%wide.region_0.2_spmd.clone.clone.clone.sunk | while | flops 4718595 | bytes 8917183 | solution.py:43
  118.9 3.0 multiply_reduce_fusion.2
  122.3 3.0 multiply_reduce_fusion.2
  125.7 3.0 multiply_reduce_fusion.2
  129.1 3.0 multiply_reduce_fusion.2
  132.5 3.0 multiply_reduce_fusion.2
  135.9 3.0 multiply_reduce_fusion.2
  139.4 3.0 multiply_reduce_fusion.2
  142.8 3.0 multiply_reduce_fusion.2
  146.2 3.0 multiply_reduce_fusion.2
  149.6 3.0 multiply_reduce_fusion.2
  153.0 3.0 multiply_reduce_fusion.2
  156.4 3.0 multiply_reduce_fusion.2
  159.9 3.0 multiply_reduce_fusion.2
  163.3 3.0 multiply_reduce_fusion.2
  166.7 3.0 multiply_reduce_fusion.2
  170.1 3.0 multiply_reduce_fusion.2
  173.1 2.5 copy.78
  175.6 3.7 copy.71
  179.2 3.4 fusion.39
  182.6 2.0 fusion.43
  184.7 2.1 fusion.41
  186.7 2.1 fusion.44
  188.8 28.8 %while.42 = (s32[]{:T(128)}, f32[2,16,512]{2,1,0:T(8,128)S(1)}, s32[]{:T(128)}, f32[32,2,16]{2,1,0:T(2,128)S(1)}, f32[32,2,16,512]{3,2,1,0:T(8,128)}, /*index=5*/s32[]{:T(128)}, s32[]{:T(128)}, s32[]{:T(128)}, s32[]{:T(128)}) while((s32[]{:T(128)}, f32[2,16,512]{2,1,0:T(8,128)S(1)}, s32[]{:T(128)}, f32[32,2,16]{2,1,0:T(2,128)S(1)}, ...), condition=%wide.region_6.7_spmd, body=%wide.region_5.6_spmd.sunk | while | flops 32774 | bytes 197147 | solution.py:24
  188.9 0.9 bitcast_add_fusion.6
  189.8 0.9 bitcast_add_fusion.6
  190.7 0.9 bitcast_add_fusion.6
  191.7 0.9 bitcast_add_fusion.6
  192.6 0.9 bitcast_add_fusion.6
  193.5 0.9 bitcast_add_fusion.6
  194.4 0.9 bitcast_add_fusion.6
  195.4 0.9 bitcast_add_fusion.6
  199.1 0.9 bitcast_add_fusion.6
  200.0 0.9 bitcast_add_fusion.6
  200.9 0.9 bitcast_add_fusion.6
  208.3 0.9 bitcast_add_fusion.6
  214.8 0.9 bitcast_add_fusion.6
  217.6 5.5 %add_bitcast_fusion = f32[512,2,512]{0,2,1:T(8,128)} fusion(f32[2,512,512]{2,1,0:T(8,128)} %fusion.39, f32[2,512,512]{2,1,0:T(8,128)} %fusion.43, f32[2,16,512]{2,1,0:T(8,128)S(1)} %get-tuple-element.178, f32[512]{0:T(512)S(1)} %fusion.35, f32[2,16]{1,0:T(2,128)S(1)} %constant_dynamic-slice_fusion.1, f32[2,16]{1,0:T(2,128)S(1)} %get-tuple-element.294), kind=kOutput, calls=%fused_computation.21 | convolution fusion | flops 101744640 | bytes 6359296 | tf_op jit(solution)/shard_map/gmb,gmc->bgc/dot_general | solution.py:82
  223.1 1.9 all_to_all.62
  225.0 1.5 copy.81
  226.5 18.8 %all-to-all-start.3 = ((f32[4,128,1024]{1,2,0:T(8,128)}), f32[4,128,1024]{1,2,0:T(8,128)S(1)}, u32[]{:S(2)}, u32[]{:S(2)}) async-start(f32[4,128,1024]{1,2,0:T(8,128)} %copy.81), calls=%async_computation.3 | async-start | bytes 4194304 | tf_op jit(solution)/shard_map/all_to_all | solution.py:131
  245.3 77.5 %all-gather.7.cloned.1.call-done = f32[64,16,512]{2,1,0:T(8,128)} async-done(((f32[2,16,512]{2,1,0:T(8,128)}), f32[64,16,512]{2,1,0:T(8,128)}) %all-gather.7.cloned.1.call-update) | async-done | bytes 2097168 | tf_op jit(solution)/shard_map/all_gather | solution.py:15
  322.9 5.5 %add_bitcast_fusion.1 = f32[512,2,512]{0,2,1:T(8,128)} fusion(f32[2,512,512]{2,1,0:T(8,128)} %fusion.41, f32[2,512,512]{2,1,0:T(8,128)} %fusion.44, f32[2,16,512]{2,1,0:T(8,128)S(1)} %get-tuple-element.177, f32[512]{0:T(512)S(1)} %fusion.33, f32[2,16]{1,0:T(2,128)S(1)} %constant_dynamic-slice_fusion.1, f32[2,16]{1,0:T(2,128)S(1)} %get-tuple-element.294), kind=kOutput, calls=%fused_computation.22 | convolution fusion | flops 101744640 | bytes 6359296 | tf_op jit(solution)/shard_map/gma,gmc->agc/dot_general | solution.py:79
  328.4 2.9 all_to_all.58
  331.2 3.0 copy.75
  334.3 26.2 %all-to-all-start.2 = ((f32[4,128,1024]{1,2,0:T(8,128)}), f32[4,128,1024]{1,2,0:T(8,128)}, u32[]{:S(2)}, u32[]{:S(2)}) async-start(f32[4,128,1024]{1,2,0:T(8,128)} %copy.75), calls=%async_computation.2 | async-start | bytes 4194304 | tf_op jit(solution)/shard_map/all_to_all | solution.py:130
  360.6 1.0 fusion.6
  361.6 110.7 %psum.7 = f32[8,16]{1,0:T(8,128)S(1)} all-reduce(f32[8,16]{1,0:T(8,128)S(1)} %fusion.36), channel_id=1, replica_groups=mesh['ctx'=32,'grp'=4] {'ctx','grp'}, use_global_device_ids=true, to_apply=%region_8.9 | all-reduce | flops 128 | bytes 1024 | tf_op jit(solution)/shard_map/psum | solution.py:144
  472.9 1.8 copy.82
  474.8 3.0 copy.76
  477.8 6.3 %convert_multiply_fusion = (f32[128,4096]{1,0:T(8,128)}, f32[128,4096]{1,0:T(8,128)}, f32[128,4096]{1,0:T(8,128)}, f32[128,4096]{1,0:T(8,128)}) fusion(f32[128,4096]{1,0:T(8,128)} %copy.76, bf16[128,4096]{1,0:T(8,128)(2,1)} %param.15, bf16[128,4096]{1,0:T(8,128)(2,1)} %param.12, f32[128,4096]{1,0:T(8,128)S(1)} %copy-done.3, ...), kind=kLoop, calls=%fused_computation.13 | loop fusion | flops 4194304 | bytes 16777216 | tf_op jit(solution)/shard_map/mul | solution.py:94
  (154 shorter events, 25.5 us)
Async XLA Ops:
  7.2 34.5 %copy-start = (f32[8,16]{1,0:T(8,128)S(1)}, f32[8,16]{1,0:T(8,128)}, u32[]{:S(2)}) copy-start(f32[8,16]{1,0:T(8,128)} %param.16) | copy-start | bytes 1540
  10.0 21.1 %all-to-all-start.1 = ((bf16[128,4,1024]{2,0,1:T(8,128)(2,1)}), bf16[128,4,1024]{2,0,1:T(8,128)(2,1)S(1)}, u32[]{:S(2)}, u32[]{:S(2)}) async-start(bf16[128,4,1024]{2,0,1:T(8,128)(2,1)} %bitcast.53), calls=%async_computation.1 | async-start | bytes 2097152 | tf_op jit(solution)/shard_map/all_to_all | solution.py:112
  16.0 19.1 %copy-start.4 = (bf16[128,4096]{1,0:T(8,128)(2,1)S(1)}, bf16[128,4096]{1,0:T(8,128)(2,1)}, u32[]{:S(2)}) copy-start(bf16[128,4096]{1,0:T(8,128)(2,1)} %param.14) | copy-start | bytes 3145732
  16.0 19.2 %copy-start.6 = (bf16[128,4096]{1,0:T(8,128)(2,1)S(1)}, bf16[128,4096]{1,0:T(8,128)(2,1)}, u32[]{:S(2)}) copy-start(bf16[128,4096]{1,0:T(8,128)(2,1)} %param.13) | copy-start | bytes 3145732
  16.0 172.8 %all-gather.9.cloned.1.call-start = ((), (), s32[]{:S(2)}) async-start(), calls=%async_computation.5 | async-start | bytes 2162688 | tf_op jit(solution)/shard_map/all_gather | solution.py:15
  31.1 1.0 copy-start.7
  36.5 73.6 %all-to-all-start = ((bf16[128,4,1024]{2,0,1:T(8,128)(2,1)}), bf16[128,4,1024]{2,0,1:T(8,128)(2,1)}, u32[]{:S(2)}, u32[]{:S(2)}) async-start(bf16[128,4,1024]{2,0,1:T(8,128)(2,1)} %bitcast.54), calls=%async_computation | async-start | bytes 2097152 | tf_op jit(solution)/shard_map/all_to_all | solution.py:111
  41.6 281.3 %all-gather.7.cloned.1.call-start = ((), (), s32[]{:S(2)}) async-start(), calls=%async_computation.4 | async-start | bytes 2162688 | tf_op jit(solution)/shard_map/all_gather | solution.py:15
  179.2 3.4 copy-start.2
  182.6 2.1 copy-start.1
  226.5 107.8 %all-to-all-start.3 = ((f32[4,128,1024]{1,2,0:T(8,128)}), f32[4,128,1024]{1,2,0:T(8,128)S(1)}, u32[]{:S(2)}, u32[]{:S(2)}) async-start(f32[4,128,1024]{1,2,0:T(8,128)} %copy.81), calls=%async_computation.3 | async-start | bytes 4194304 | tf_op jit(solution)/shard_map/all_to_all | solution.py:131
  334.3 140.5 %all-to-all-start.2 = ((f32[4,128,1024]{1,2,0:T(8,128)}), f32[4,128,1024]{1,2,0:T(8,128)}, u32[]{:S(2)}, u32[]{:S(2)}) async-start(f32[4,128,1024]{1,2,0:T(8,128)} %copy.75), calls=%async_computation.2 | async-start | bytes 4194304 | tf_op jit(solution)/shard_map/all_to_all | solution.py:130
  474.8 3.0 copy-start.3
  474.8 3.0 copy-start.5
Sparse Core Ops, SparseCore 0:
  35.3 132.3 all-gather.8
  169.3 153.5 all-gather.6
where the time goes:
time: 494 us; the launch traced here: 491 us
  blocking collectives  179 us (36%)
  other arithmetic  91.8 us (19%)
  waiting for transfers between devices  91.8 us (19%)
  starting transfers between devices  56.1 us (11%)
  local copies, waits for them, and re-layouts  28.8 us (6%)
  matrix products  28.5 us (6%)
  between operations  14.1 us (3%)
    psum x1, blocking collectives, on_device(): summed = lax.psum(placed, ('ctx', 'grp'))  111 us
    all_gather x2, waiting for transfers between devices, entering(): gathered = jax.tree.map(lambda a: lax.all_gather(a, axis), part)  77.6 us
    all_gather x1, blocking collectives, entering(): gathered = jax.tree.map(lambda a: lax.all_gather(a, axis), part)  68.3 us
    reduce_sum x16, other arithmetic, one_mode(): return (total, jnp.sum(pairing * weight, axis=(1, 2)))  47.3 us
    add x31, other arithmetic, link_states(): return (later[1][:, :, None] * earlier[0] + later[0], earlier[1] * later[1])  28.6 us
    all_to_all x1, starting transfers between devices, channel_layout(): lax.all_to_all(mixed_cols, 'grp', split_axis=0, concat_axis=1, tiled=True)  26.2 us
    all_to_all x1, starting transfers between devices, channel_layout(): lax.all_to_all(conv_cols, 'grp', split_axis=0, concat_axis=1, tiled=True)  18.8 us
    all_to_all x1, waiting for transfers between devices, channel_layout(): lax.all_to_all(inner_grad, 'grp', split_axis=1, concat_axis=0, tiled=True)  14.2 us
  transfers between devices with their start and end apart: 6, of which 2 were waited for; matrix products, arithmetic and copies ran while one was open for 26% of the time, Pallas kernels for 0%

commit v1 on v0

--- a/solution.py
+++ b/solution.py
@@ -141,7 +141,9 @@
     results, placed, length = channel_layout(
         query_input, key_input, value_input, out_grad, residues, decay_rates
     )
-    summed = lax.psum(placed, ("ctx", "grp"))
+    summed = placed
+    for j0 in ("grp", "ctx"):
+        summed = jax.lax.psum(summed, axis_name=j0)
     residue_grad = summed / (length * math.sqrt(GROUP))
     return (results[0], results[1], results[2], results[3], residue_grad)
 

time: 494 us -> 521 us (1.055)
  the two profiles are of different devices: /device:TPU:1 before, /device:TPU:16 now
where the time goes in v1:
time: 521 us; the launch traced here: 518 us
  blocking collectives  221 us (42%)
  waiting for transfers between devices  111 us (21%)
  other arithmetic  91.9 us (18%)
  local copies, waits for them, and re-layouts  28.8 us (6%)
  matrix products  28.4 us (5%)
  starting transfers between devices  22.3 us (4%)
  between operations  14.1 us (3%)
    psum x2, blocking collectives, on_device(): summed = jax.lax.psum(summed, axis_name=j0)  139 us
    all_gather x2, waiting for transfers between devices, entering(): gathered = jax.tree.map(lambda a: lax.all_gather(a, axis), part)  98.5 us
    all_gather x1, blocking collectives, entering(): gathered = jax.tree.map(lambda a: lax.all_gather(a, axis), part)  82.3 us
    reduce_sum x16, other arithmetic, one_mode(): return (total, jnp.sum(pairing * weight, axis=(1, 2)))  47.3 us
    add x31, other arithmetic, link_states(): return (later[1][:, :, None] * earlier[0] + later[0], earlier[1] * later[1])  28.6 us
    all_to_all x1, waiting for transfers between devices, channel_layout(): lax.all_to_all(inner_grad, 'grp', split_axis=1, concat_axis=0, tiled=True)  11.9 us
  transfers between devices with their start and end apart: 6, of which 2 were waited for; matrix products, arithmetic and copies ran while one was open for 25% of the time, Pallas kernels for 0%

profile of v1, /device:TPU:16, one launch (start us, length us, event | category | flops | bytes accessed | tf_op | source)
XLA Modules:
  0.0 518.0 jit_solution(4828907622907540834)
XLA Ops:
  7.2 1.8 fusion.5
  9.0 1.1 copy.101
  10.0 4.8 all-to-all-start.1
  15.7 11.9 %all-to-all-done.1 = bf16[128,4,1024]{2,0,1:T(8,128)(2,1)S(1)} async-done(((bf16[128,4,1024]{2,0,1:T(8,128)(2,1)}), bf16[128,4,1024]{2,0,1:T(8,128)(2,1)S(1)}, u32[]{:S(2)}, u32[]{:S(2)}) %all-to-all-start.1) | async-done | bytes 1048608 | tf_op jit(solution)/shard_map/all_to_all | solution.py:112
  27.6 1.0 copy-done.7
  28.6 1.8 reshape.76
  30.5 1.2 fusion.12
  31.9 1.1 copy.102
  33.0 7.4 %all-to-all-start = ((bf16[128,4,1024]{2,0,1:T(8,128)(2,1)}), bf16[128,4,1024]{2,0,1:T(8,128)(2,1)}, u32[]{:S(2)}, u32[]{:S(2)}) async-start(bf16[128,4,1024]{2,0,1:T(8,128)(2,1)} %bitcast.54), calls=%async_computation | async-start | bytes 2097152 | tf_op jit(solution)/shard_map/all_to_all | solution.py:111
  40.6 82.3 %all-gather.3 = f32[32,2,16]{2,1,0:T(2,128)S(1)} all-gather(f32[1,2,16]{2,1,0:T(2,128)S(1)} %get-tuple-element.293), channel_id=2, replica_groups=mesh['ctx'=32,'grp'=4] {'ctx'}, dimensions={0}, use_global_device_ids=true | all-gather | bytes 4224 | tf_op jit(solution)/shard_map/all_gather | solution.py:15
  122.8 2.6 reshape.75
  125.5 2.4 fusion.7
  127.9 3.3 fusion.9
  131.2 54.7 %while.43 = (s32[]{:T(128)}, f32[2,512,512]{2,1,0:T(8,128)S(1)}, f32[16,2]{1,0:T(8,128)S(1)}, f32[16,2]{1,0:T(8,128)S(1)}, f32[16,2]{1,0:T(8,128)S(1)}, /*index=...) while((s32[]{:T(128)}, f32[2,512,512]{2,1,0:T(8,128)S(1)}, ...), condition=%wide.region_2.3_spmd.clone.clone.clone, body=%wide.region_0.2_spmd.clone.clone.clone.sunk | while | flops 4718595 | bytes 8917183 | solution.py:43
  131.6 3.0 multiply_reduce_fusion.2
  135.0 3.0 multiply_reduce_fusion.2
  138.5 3.0 multiply_reduce_fusion.2
  141.9 3.0 multiply_reduce_fusion.2
  145.3 3.0 multiply_reduce_fusion.2
  148.7 3.0 multiply_reduce_fusion.2
  152.1 3.0 multiply_reduce_fusion.2
  155.6 3.0 multiply_reduce_fusion.2
  159.0 3.0 multiply_reduce_fusion.2
  162.4 3.0 multiply_reduce_fusion.2
  165.8 3.0 multiply_reduce_fusion.2
  169.3 3.0 multiply_reduce_fusion.2
  172.7 3.0 multiply_reduce_fusion.2
  176.1 3.0 multiply_reduce_fusion.2
  179.5 3.0 multiply_reduce_fusion.2
  182.9 3.0 multiply_reduce_fusion.2
  185.9 2.5 copy.78
  188.4 3.7 copy.71
  192.1 3.4 fusion.39
  195.4 2.0 fusion.43
  197.5 2.1 fusion.41
  199.6 2.1 fusion.44
  201.7 28.8 %while.42 = (s32[]{:T(128)}, f32[2,16,512]{2,1,0:T(8,128)S(1)}, s32[]{:T(128)}, f32[32,2,16]{2,1,0:T(2,128)S(1)}, f32[32,2,16,512]{3,2,1,0:T(8,128)}, /*index=5*/s32[]{:T(128)}, s32[]{:T(128)}, s32[]{:T(128)}, s32[]{:T(128)}) while((s32[]{:T(128)}, f32[2,16,512]{2,1,0:T(8,128)S(1)}, s32[]{:T(128)}, f32[32,2,16]{2,1,0:T(2,128)S(1)}, ...), condition=%wide.region_6.7_spmd, body=%wide.region_5.6_spmd.sunk | while | flops 32774 | bytes 197147 | solution.py:24
  201.7 0.9 bitcast_add_fusion.6
  202.6 0.9 bitcast_add_fusion.6
  203.6 0.9 bitcast_add_fusion.6
  208.2 0.9 bitcast_add_fusion.6
  209.1 0.9 bitcast_add_fusion.6
  210.1 0.9 bitcast_add_fusion.6
  215.6 0.9 bitcast_add_fusion.6
  218.4 0.9 bitcast_add_fusion.6
  220.3 0.9 bitcast_add_fusion.6
  221.2 0.9 bitcast_add_fusion.6
  225.8 0.9 bitcast_add_fusion.6
  228.6 0.9 bitcast_add_fusion.6
  230.4 5.5 %add_bitcast_fusion = f32[512,2,512]{0,2,1:T(8,128)} fusion(f32[2,512,512]{2,1,0:T(8,128)} %fusion.39, f32[2,512,512]{2,1,0:T(8,128)} %fusion.43, f32[2,16,512]{2,1,0:T(8,128)S(1)} %get-tuple-element.178, f32[512]{0:T(512)S(1)} %fusion.35, f32[2,16]{1,0:T(2,128)S(1)} %constant_dynamic-slice_fusion.1, f32[2,16]{1,0:T(2,128)S(1)} %get-tuple-element.294), kind=kOutput, calls=%fused_computation.21 | convolution fusion | flops 101744640 | bytes 6359296 | tf_op jit(solution)/shard_map/gmb,gmc->bgc/dot_general | solution.py:82
  235.9 1.9 all_to_all.62
  237.9 1.5 copy.81
  239.3 4.8 all-to-all-start.3
  244.1 98.5 %all-gather.7.cloned.1.call-done = f32[64,16,512]{2,1,0:T(8,128)} async-done(((f32[2,16,512]{2,1,0:T(8,128)}), f32[64,16,512]{2,1,0:T(8,128)}) %all-gather.7.cloned.1.call-update) | async-done | bytes 2097168 | tf_op jit(solution)/shard_map/all_gather | solution.py:15
  342.7 5.5 %add_bitcast_fusion.1 = f32[512,2,512]{0,2,1:T(8,128)} fusion(f32[2,512,512]{2,1,0:T(8,128)} %fusion.41, f32[2,512,512]{2,1,0:T(8,128)} %fusion.44, f32[2,16,512]{2,1,0:T(8,128)S(1)} %get-tuple-element.177, f32[512]{0:T(512)S(1)} %fusion.33, f32[2,16]{1,0:T(2,128)S(1)} %constant_dynamic-slice_fusion.1, f32[2,16]{1,0:T(2,128)S(1)} %get-tuple-element.294), kind=kOutput, calls=%fused_computation.22 | convolution fusion | flops 101744640 | bytes 6359296 | tf_op jit(solution)/shard_map/gma,gmc->agc/dot_general | solution.py:79
  348.1 2.9 all_to_all.58
  351.0 3.0 copy.75
  354.1 5.3 %all-to-all-start.2 = ((f32[4,128,1024]{1,2,0:T(8,128)}), f32[4,128,1024]{1,2,0:T(8,128)}, u32[]{:S(2)}, u32[]{:S(2)}) async-start(f32[4,128,1024]{1,2,0:T(8,128)} %copy.75), calls=%async_computation.2 | async-start | bytes 4194304 | tf_op jit(solution)/shard_map/all_to_all | solution.py:130
  359.5 1.0 fusion.6
  360.5 27.3 %psum.14 = f32[8,16]{1,0:T(8,128)S(1)} all-reduce(f32[8,16]{1,0:T(8,128)S(1)} %fusion.36), channel_id=1, replica_groups=mesh['ctx'=32,'grp'=4] {'grp'}, use_global_device_ids=true, to_apply=%region_8.9 | all-reduce | flops 128 | bytes 1024 | tf_op jit(solution)/shard_map/psum | solution.py:146
  387.8 111.6 %psum.15 = f32[8,16]{1,0:T(8,128)S(1)} all-reduce(f32[8,16]{1,0:T(8,128)S(1)} %psum.14), channel_id=1, replica_groups=mesh['ctx'=32,'grp'=4] {'ctx'}, use_global_device_ids=true, to_apply=%region_9.10 | all-reduce | flops 128 | bytes 1024 | tf_op jit(solution)/shard_map/psum | solution.py:146
  499.9 1.8 copy.82
  501.8 3.0 copy.76
  504.8 6.3 %convert_multiply_fusion = (f32[128,4096]{1,0:T(8,128)}, f32[128,4096]{1,0:T(8,128)}, f32[128,4096]{1,0:T(8,128)}, f32[128,4096]{1,0:T(8,128)}) fusion(f32[128,4096]{1,0:T(8,128)} %copy.76, bf16[128,4096]{1,0:T(8,128)(2,1)} %param.15, bf16[128,4096]{1,0:T(8,128)(2,1)} %param.12, f32[128,4096]{1,0:T(8,128)S(1)} %copy-done.3, ...), kind=kLoop, calls=%fused_computation.13 | loop fusion | flops 4194304 | bytes 16777216 | tf_op jit(solution)/shard_map/mul | solution.py:94
  (155 shorter events, 26.4 us)
Async XLA Ops:
  7.2 33.3 %copy-start = (f32[8,16]{1,0:T(8,128)S(1)}, f32[8,16]{1,0:T(8,128)}, u32[]{:S(2)}) copy-start(f32[8,16]{1,0:T(8,128)} %param.16) | copy-start | bytes 1540
  10.0 17.6 %all-to-all-start.1 = ((bf16[128,4,1024]{2,0,1:T(8,128)(2,1)}), bf16[128,4,1024]{2,0,1:T(8,128)(2,1)S(1)}, u32[]{:S(2)}, u32[]{:S(2)}) async-start(bf16[128,4,1024]{2,0,1:T(8,128)(2,1)} %bitcast.53), calls=%async_computation.1 | async-start | bytes 2097152 | tf_op jit(solution)/shard_map/all_to_all | solution.py:112
  14.8 16.8 %copy-start.4 = (bf16[128,4096]{1,0:T(8,128)(2,1)S(1)}, bf16[128,4096]{1,0:T(8,128)(2,1)}, u32[]{:S(2)}) copy-start(bf16[128,4096]{1,0:T(8,128)(2,1)} %param.14) | copy-start | bytes 3145732
  14.8 16.8 %copy-start.6 = (bf16[128,4096]{1,0:T(8,128)(2,1)S(1)}, bf16[128,4096]{1,0:T(8,128)(2,1)}, u32[]{:S(2)}) copy-start(bf16[128,4096]{1,0:T(8,128)(2,1)} %param.13) | copy-start | bytes 3145732
  14.8 186.8 %all-gather.9.cloned.1.call-start = ((), (), s32[]{:S(2)}) async-start(), calls=%async_computation.5 | async-start | bytes 2162688 | tf_op jit(solution)/shard_map/all_gather | solution.py:15
  27.6 1.0 copy-start.7
  33.0 89.8 %all-to-all-start = ((bf16[128,4,1024]{2,0,1:T(8,128)(2,1)}), bf16[128,4,1024]{2,0,1:T(8,128)(2,1)}, u32[]{:S(2)}, u32[]{:S(2)}) async-start(bf16[128,4,1024]{2,0,1:T(8,128)(2,1)} %bitcast.54), calls=%async_computation | async-start | bytes 2097152 | tf_op jit(solution)/shard_map/all_to_all | solution.py:111
  40.4 302.3 %all-gather.7.cloned.1.call-start = ((), (), s32[]{:S(2)}) async-start(), calls=%async_computation.4 | async-start | bytes 2162688 | tf_op jit(solution)/shard_map/all_gather | solution.py:15
  192.1 3.4 copy-start.2
  195.4 2.1 copy-start.1
  239.3 114.7 %all-to-all-start.3 = ((f32[4,128,1024]{1,2,0:T(8,128)}), f32[4,128,1024]{1,2,0:T(8,128)S(1)}, u32[]{:S(2)}, u32[]{:S(2)}) async-start(f32[4,128,1024]{1,2,0:T(8,128)} %copy.81), calls=%async_computation.3 | async-start | bytes 4194304 | tf_op jit(solution)/shard_map/all_to_all | solution.py:131
  354.1 147.7 %all-to-all-start.2 = ((f32[4,128,1024]{1,2,0:T(8,128)}), f32[4,128,1024]{1,2,0:T(8,128)}, u32[]{:S(2)}, u32[]{:S(2)}) async-start(f32[4,128,1024]{1,2,0:T(8,128)} %copy.75), calls=%async_computation.2 | async-start | bytes 4194304 | tf_op jit(solution)/shard_map/all_to_all | solution.py:130
  501.8 3.0 copy-start.3
  501.8 3.0 copy-start.5
Sparse Core Ops, SparseCore 0:
  31.8 155.5 all-gather.8
  189.1 153.5 all-gather.6
